TPU v7x, 32 devices: a whole 2x2x4 slice. The times are simulated.
32 devices in a mesh: cube: 16 (over z, y, x), front: 2 (over core).
Axes of the slice: x: 2, y: 2, z: 4, core: 2. Of those that a mesh axis runs over, the one named last changes fastest.
Arguments:
- elem_loads: float32 [64, 8192], P(None, ('cube', 'front')), may hold values from -6 to 6
- elem_owner: int32 [8192, 1], P(('cube', 'front')), may hold values from 0 to 31; in each aligned block of 256 rows (0 to 255, 256 to 511, ...) at most 16 rows name the same one
- elem_row: int32 [8192], P(('cube', 'front')), may hold values from 0 to 1023
- sep_loads: float32 [4, 64, 512], P(None, None, ('cube', 'front')), may hold values from -6 to 6
- leaf_inverse: float32 [32768, 1024], P(('cube', 'front'))
- leaf_coupling: float32 [64, 32768], P(None, ('cube', 'front')), may hold values from -0.09375 to 0.09375
- coupling0: float32 [512, 512], P(None, ('cube', 'front')), may hold values from -0.25 to 0.25
- coupling1: float32 [256, 512], P(None, ('cube', 'front')), may hold values from -0.375 to 0.375
- coupling2: float32 [128, 512], P(None, ('cube', 'front')), may hold values from -0.5 to 0.5
- inverse0: float32 [512, 512], P(('cube', 'front'))
- inverse1: float32 [512, 256], P(('cube', 'front'))
- inverse2: float32 [512, 128], P(('cube', 'front'))
- inverse3: float32 [512, 64], P(('cube', 'front'))
Outputs:
- leaf_solution: float32 [64, 32768], P(None, ('cube', 'front'))
- sep_solution: float32 [4, 64, 512], P(None, None, ('cube', 'front'))
Inputs may be any that keep to these rules, and one draw needn't show every extreme that they name: `elem_owner`: among the element rows of one device, at most 16 name the same owner, a bound that some block reaches.
All inputs are finite; a program needn't handle non-finite values.
Results may differ from a plain program's by a relative error of at most 0.00012.
Values sent between devices are 32-bit elements; how exact they have to be, the bound alone decides.
A program may use at most 64 MiB of HBM per device.

v0:
```python
import jax
import jax.numpy as jnp
from jax import lax
from jax.sharding import PartitionSpec as P

HIGH = lax.Precision.HIGHEST


def partner(block, axis, apart):
    count = lax.axis_size(axis)
    route = []
    for low in range(count):
        high = low | 1 << apart
        if high != low and high < count:
            route += [(low, high), (high, low)]
    return lax.ppermute(block, axis, route)


def row_dot(left, right):
    return lax.dot_general(left, right, (((1,), (1,)), ((), ())), precision=HIGH)


def mat_dot(left, right):
    return jnp.dot(left, right, precision=HIGH)


def reduce_rows(term, group, position):
    current = term
    for bit in reversed(range(group.bit_length() - 1)):
        half = current.shape[1] // 2
        lower, upper = (current[:, :half], current[:, half:])
        mine = position >> bit & 1 == 1
        keep = jnp.where(mine, upper, lower)
        leave = jnp.where(mine, lower, upper)
        current = keep + partner(leave, ("cube", "front"), bit)
    return current


def gather_rows(local, group, position):
    current = local
    for bit in range(group.bit_length() - 1):
        other = partner(current, ("cube", "front"), bit)
        mine = position >> bit & 1 == 1
        current = jnp.where(
            mine, jnp.concatenate([other, current], 1), jnp.concatenate([current, other], 1)
        )
    return current


def total_rows(term, group):
    current = term
    for bit in range(group.bit_length() - 1):
        current = current + partner(current, ("cube", "front"), bit)
    return current


def shards(
    elem_loads,
    elem_owner,
    elem_row,
    sep_loads,
    leaf_inverse,
    leaf_coupling,
    coupling0,
    coupling1,
    coupling2,
    inverse0,
    inverse1,
    inverse2,
    inverse3,
):
    position = lax.axis_index(("cube", "front"))
    devices = lax.axis_size(("cube", "front"))
    columns = elem_loads.shape[0]
    leaf_rows = leaf_inverse.shape[0]
    sep_rows = sep_loads.shape[2]
    count = elem_owner.shape[0]
    capacity = 2 * count // devices
    owner = elem_owner[:, 0]
    marks = (owner[:, None] == jnp.arange(devices, dtype=jnp.int32)[None, :]).astype(jnp.int32)
    ranks = jnp.sum(jnp.cumsum(marks, axis=0) * marks, axis=1) - 1
    slots = owner * capacity + ranks
    send_vals = jnp.zeros((columns, devices * capacity), jnp.float32).at[:, slots].set(elem_loads)
    send_rows = jnp.full((1, devices * capacity), -1, jnp.int32).at[0, slots].set(elem_row)
    got_vals, got_rows = (
        lax.all_to_all(send_vals, ("cube", "front"), split_axis=1, concat_axis=1, tiled=True),
        lax.all_to_all(send_rows, ("cube", "front"), split_axis=1, concat_axis=1, tiled=True),
    )
    placing = (got_rows[0][:, None] == jnp.arange(leaf_rows, dtype=jnp.int32)[None, :]).astype(
        jnp.float32
    )
    loads = mat_dot(got_vals, placing)
    leaf_y = row_dot(loads, leaf_inverse)
    inverses = [inverse0, inverse1, inverse2, inverse3]
    couplings = [coupling0, coupling1, coupling2, leaf_coupling]
    sep_y = [None] * 4
    child = leaf_y
    for level in (3, 2, 1, 0):
        group = devices >> level
        term = row_dot(child, couplings[level])
        resid = sep_loads[level] - reduce_rows(term, group, position)
        sep_y[level] = row_dot(gather_rows(resid, group, position), inverses[level])
        child = sep_y[level]
    solved = []
    parent = None
    for level in range(4):
        group = devices >> level
        upper = sep_y[level]
        if level > 0:
            upper = upper - mat_dot(parent, couplings[level - 1])
        term = mat_dot(upper, inverses[level])
        parent = total_rows(term, group)
        mine = lax.dynamic_slice_in_dim(parent, position % group * sep_rows, sep_rows, 1)
        solved.append(mine)
    upper = leaf_y - mat_dot(parent, leaf_coupling)
    leaf_solution = mat_dot(upper, leaf_inverse)
    return (leaf_solution, jnp.stack(solved))


def solution(mesh):
    in_specs = (
        P(None, ("cube", "front")),
        P(("cube", "front"), None),
        P(("cube", "front")),
        P(None, None, ("cube", "front")),
        P(("cube", "front"), None),
        P(None, ("cube", "front")),
        P(None, ("cube", "front")),
        P(None, ("cube", "front")),
        P(None, ("cube", "front")),
        P(("cube", "front"), None),
        P(("cube", "front"), None),
        P(("cube", "front"), None),
        P(("cube", "front"), None),
    )
    out_specs = (P(None, ("cube", "front")), P(None, None, ("cube", "front")))
    return jax.shard_map(shards, mesh=mesh, in_specs=in_specs, out_specs=out_specs, check_vma=False)
```

profile of v0, /device:TPU:0, one launch (start us, length us, event | category | flops | bytes accessed | tf_op | source)
XLA Modules:
  0.0 199.2 jit_solution(2309752474257731399)
XLA Ops:
  5.9 7.3 %all-to-all-start.1 = ((s32[1,32,16]{2,0,1:T(1,128)}), s32[1,32,16]{2,0,1:T(1,128)S(1)}, u32[]{:S(2)}, u32[]{:S(2)}) async-start(s32[1,32,16]{2,0,1:T(1,128)} %bitcast.8), calls=%async_computation.1 | async-start | bytes 32768 | tf_op jit(solution)/shard_map/all_to_all | solution.py:87
  16.3 4.1 %all-to-all-done.1 = s32[1,32,16]{2,0,1:T(1,128)S(1)} async-done(((s32[1,32,16]{2,0,1:T(1,128)}), s32[1,32,16]{2,0,1:T(1,128)S(1)}, u32[]{:S(2)}, u32[]{:S(2)}) %all-to-all-start.1) | async-done | bytes 2080 | tf_op jit(solution)/shard_map/all_to_all | solution.py:87
  24.4 6.7 %all-to-all-done = f32[32,1,1024]{2,1,0:T(1,128)S(1)} async-done(((f32[32,1,1024]{2,1,0:T(1,128)}), f32[32,1,1024]{2,1,0:T(1,128)S(1)}, u32[]{:S(2)}, u32[]{:S(2)}) %all-to-all-start) | async-done | bytes 131104 | tf_op jit(solution)/shard_map/all_to_all | solution.py:86
  33.7 6.3 %fusion.41 = f32[64,1024]{1,0:T(8,128)S(1)} fusion(f32[64,1024]{1,0:T(8,128)S(1)} %fusion, f32[1024,1024]{1,0:T(8,128)} %param.17), kind=kOutput, calls=%fused_computation.102 | convolution fusion | flops 805306368 | bytes 4718592 | tf_op jit(solution)/shard_map/dot_general | solution.py:20
  40.8 3.4 %collective-permute-done = f32[64,32]{0,1:T(8,128)S(1)} collective-permute-done((f32[64,32]{0,1:T(8,128)S(1)}, f32[64,32]{0,1:T(8,128)S(1)}, u32[]{:S(2)}, u32[]{:S(2)}) %collective-permute-start) | collective-permute-done | bytes 8224 | tf_op jit(solution)/shard_map/ppermute | solution.py:16
  55.3 3.4 %collective-permute-done.5 = f32[64,32]{0,1:T(8,128)S(1)} collective-permute-done((f32[64,32]{0,1:T(8,128)S(1)}, f32[64,32]{0,1:T(8,128)S(1)}, u32[]{:S(2)}, u32[]{:S(2)}) %collective-permute-start.5) | collective-permute-done | bytes 8224 | tf_op jit(solution)/shard_map/ppermute | solution.py:16
  61.5 3.4 %collective-permute-done.8 = f32[64,32]{0,1:T(8,128)S(1)} collective-permute-done((f32[64,32]{0,1:T(8,128)S(1)}, f32[64,32]{0,1:T(8,128)S(1)}, u32[]{:S(2)}, u32[]{:S(2)}) %collective-permute-start.8) | collective-permute-done | bytes 8224 | tf_op jit(solution)/shard_map/ppermute | solution.py:16
  70.1 3.6 %collective-permute-done.10 = f32[64,128]{0,1:T(8,128)S(1)} collective-permute-done((f32[64,128]{0,1:T(8,128)S(1)}, f32[64,128]{0,1:T(8,128)S(1)}, u32[]{:S(2)}, u32[]{:S(2)}) %collective-permute-start.10) | collective-permute-done | bytes 32800 | tf_op jit(solution)/shard_map/ppermute | solution.py:16
  78.2 3.4 %collective-permute-done.12 = f32[64,32]{0,1:T(8,128)S(1)} collective-permute-done((f32[64,32]{0,1:T(8,128)S(1)}, f32[64,32]{0,1:T(8,128)S(1)}, u32[]{:S(2)}, u32[]{:S(2)}) %collective-permute-start.12) | collective-permute-done | bytes 8224 | tf_op jit(solution)/shard_map/ppermute | solution.py:16
  84.3 3.4 %collective-permute-done.15 = f32[64,32]{0,1:T(8,128)S(1)} collective-permute-done((f32[64,32]{0,1:T(8,128)S(1)}, f32[64,32]{0,1:T(8,128)S(1)}, u32[]{:S(2)}, u32[]{:S(2)}) %collective-permute-start.15) | collective-permute-done | bytes 8224 | tf_op jit(solution)/shard_map/ppermute | solution.py:16
  92.4 3.6 %collective-permute-done.17 = f32[64,128]{0,1:T(8,128)S(1)} collective-permute-done((f32[64,128]{0,1:T(8,128)S(1)}, f32[64,128]{0,1:T(8,128)S(1)}, u32[]{:S(2)}, u32[]{:S(2)}) %collective-permute-start.17) | collective-permute-done | bytes 32800 | tf_op jit(solution)/shard_map/ppermute | solution.py:16
  97.7 6.5 %collective-permute-done.18 = f32[64,256]{0,1:T(8,128)S(1)} collective-permute-done((f32[64,256]{0,1:T(8,128)S(1)}, f32[64,256]{0,1:T(8,128)S(1)}, u32[]{:S(2)}, u32[]{:S(2)}) %collective-permute-start.18) | collective-permute-done | bytes 65568 | tf_op jit(solution)/shard_map/ppermute | solution.py:16
  104.3 4.3 %collective-permute-done.19 = f32[64,128]{0,1:T(8,128)S(1)} collective-permute-done((f32[64,128]{0,1:T(8,128)S(1)}, f32[64,128]{0,1:T(8,128)S(1)}, u32[]{:S(2)}, u32[]{:S(2)}) %collective-permute-start.19) | collective-permute-done | bytes 32800 | tf_op jit(solution)/shard_map/ppermute | solution.py:16
  126.6 4.3 %collective-permute-done.26 = f32[64,128]{0,1:T(8,128)S(1)} collective-permute-done((f32[64,128]{0,1:T(8,128)S(1)}, f32[64,128]{0,1:T(8,128)S(1)}, u32[]{:S(2)}, u32[]{:S(2)}) %collective-permute-start.26) | collective-permute-done | bytes 32800 | tf_op jit(solution)/shard_map/ppermute | solution.py:16
  131.0 7.0 %collective-permute-done.27 = f32[64,256]{0,1:T(8,128)S(1)} collective-permute-done((f32[64,256]{0,1:T(8,128)S(1)}, f32[64,256]{0,1:T(8,128)S(1)}, u32[]{:S(2)}, u32[]{:S(2)}) %collective-permute-start.27) | collective-permute-done | bytes 65568 | tf_op jit(solution)/shard_map/ppermute | solution.py:16
  140.5 5.2 %collective-permute-done.29 = f32[64,512]{1,0:T(8,128)S(1)} collective-permute-done((f32[64,512]{1,0:T(8,128)S(1)}, f32[64,512]{1,0:T(8,128)S(1)}, u32[]{:S(2)}, u32[]{:S(2)}) %collective-permute-start.29) | collective-permute-done | bytes 131104 | tf_op jit(solution)/shard_map/ppermute | solution.py:16
  146.4 4.3 %collective-permute-done.30 = f32[64,512]{1,0:T(8,128)S(1)} collective-permute-done((f32[64,512]{1,0:T(8,128)S(1)}, f32[64,512]{1,0:T(8,128)S(1)}, u32[]{:S(2)}, u32[]{:S(2)}) %collective-permute-start.30) | collective-permute-done | bytes 131104 | tf_op jit(solution)/shard_map/ppermute | solution.py:16
  150.8 5.0 %collective-permute-done.31 = f32[64,512]{1,0:T(8,128)S(1)} collective-permute-done((f32[64,512]{1,0:T(8,128)S(1)}, f32[64,512]{1,0:T(8,128)S(1)}, u32[]{:S(2)}, u32[]{:S(2)}) %collective-permute-start.31) | collective-permute-done | bytes 131104 | tf_op jit(solution)/shard_map/ppermute | solution.py:16
  155.9 6.7 %collective-permute-done.32 = f32[64,512]{1,0:T(8,128)S(1)} collective-permute-done((f32[64,512]{1,0:T(8,128)S(1)}, f32[64,512]{1,0:T(8,128)S(1)}, u32[]{:S(2)}, u32[]{:S(2)}) %collective-permute-start.32) | collective-permute-done | bytes 131104 | tf_op jit(solution)/shard_map/ppermute | solution.py:16
  164.9 3.9 %collective-permute-done.34 = f32[64,256]{1,0:T(8,128)S(1)} collective-permute-done((f32[64,256]{1,0:T(8,128)S(1)}, f32[64,256]{1,0:T(8,128)S(1)}, u32[]{:S(2)}, u32[]{:S(2)}) %collective-permute-start.34) | collective-permute-done | bytes 65568 | tf_op jit(solution)/shard_map/ppermute | solution.py:16
  169.5 3.6 %collective-permute-done.35 = f32[64,256]{1,0:T(8,128)S(1)} collective-permute-done((f32[64,256]{1,0:T(8,128)S(1)}, f32[64,256]{1,0:T(8,128)S(1)}, u32[]{:S(2)}, u32[]{:S(2)}) %collective-permute-start.35) | collective-permute-done | bytes 65568 | tf_op jit(solution)/shard_map/ppermute | solution.py:16
  173.2 4.3 %collective-permute-done.36 = f32[64,256]{1,0:T(8,128)S(1)} collective-permute-done((f32[64,256]{1,0:T(8,128)S(1)}, f32[64,256]{1,0:T(8,128)S(1)}, u32[]{:S(2)}, u32[]{:S(2)}) %collective-permute-start.36) | collective-permute-done | bytes 65568 | tf_op jit(solution)/shard_map/ppermute | solution.py:16
  179.6 3.5 %collective-permute-done.38 = f32[64,128]{1,0:T(8,128)S(1)} collective-permute-done((f32[64,128]{1,0:T(8,128)S(1)}, f32[64,128]{1,0:T(8,128)S(1)}, u32[]{:S(2)}, u32[]{:S(2)}) %collective-permute-start.38) | collective-permute-done | bytes 32800 | tf_op jit(solution)/shard_map/ppermute | solution.py:16
  193.1 5.5 %fusion.50 = f32[64,1024]{1,0:T(8,128)} fusion(f32[64,1024]{1,0:T(8,128)S(1)} %convolution_subtract_fusion, f32[1024,1024]{1,0:T(8,128)} %param.17), kind=kOutput, calls=%fused_computation.111 | convolution fusion | flops 805306368 | bytes 4718592 | tf_op jit(solution)/shard_map/dot_general | solution.py:24
  (180 shorter events, 85.4 us)
Async XLA Ops:
  5.9 14.4 %all-to-all-start.1 = ((s32[1,32,16]{2,0,1:T(1,128)}), s32[1,32,16]{2,0,1:T(1,128)S(1)}, u32[]{:S(2)}, u32[]{:S(2)}) async-start(s32[1,32,16]{2,0,1:T(1,128)} %bitcast.8), calls=%async_computation.1 | async-start | bytes 32768 | tf_op jit(solution)/shard_map/all_to_all | solution.py:87
  20.4 10.8 %all-to-all-start = ((f32[32,1,1024]{2,1,0:T(1,128)}), f32[32,1,1024]{2,1,0:T(1,128)S(1)}, u32[]{:S(2)}, u32[]{:S(2)}) async-start(f32[32,1,1024]{2,1,0:T(1,128)} %reshape.69), calls=%async_computation | async-start | bytes 262144 | tf_op jit(solution)/shard_map/all_to_all | solution.py:86
  50.9 4.0 %collective-permute-start.4 = (f32[64,64]{0,1:T(8,128)S(1)}, f32[64,64]{0,1:T(8,128)S(1)}, u32[]{:S(2)}, u32[]{:S(2)}) collective-permute-start(f32[64,64]{0,1:T(8,128)S(1)} %slice_select_fusion.5), channel_id=1, source_target_pairs={{0,4},{4,0},{1,5},{5,1},{2,6},{6,2},{3,7},{7,3},{8,12},{12,8},{9,1... | collective-permute-start | bytes 49160 | tf_op jit(solution)/shard_map/ppermute | solution.py:16
  64.9 3.9 %collective-permute-start.9 = (f32[64,64]{0,1:T(8,128)S(1)}, f32[64,64]{0,1:T(8,128)S(1)}, u32[]{:S(2)}, u32[]{:S(2)}) collective-permute-start(f32[64,64]{0,1:T(8,128)S(1)} %maximum_select_fusion.11), channel_id=1, source_target_pairs={{0,4},{4,0},{1,5},{5,1},{2,6},{6,2},{3,7},{7,3},{8,12},{12,8},{9,1... | collective-permute-start | bytes 49160 | tf_op jit(solution)/shard_map/ppermute | solution.py:16
  69.4 4.3 %collective-permute-start.10 = (f32[64,128]{0,1:T(8,128)S(1)}, f32[64,128]{0,1:T(8,128)S(1)}, u32[]{:S(2)}, u32[]{:S(2)}) collective-permute-start(f32[64,128]{0,1:T(8,128)S(1)} %slice_select_fusion.2), channel_id=1, source_target_pairs={{0,8},{8,0},{1,9},{9,1},{2,10},{10,2},{3,11},{11,3},{4,12},{12,4},... | collective-permute-start | bytes 98312 | tf_op jit(solution)/shard_map/ppermute | solution.py:16
  73.8 4.0 %collective-permute-start.11 = (f32[64,64]{0,1:T(8,128)S(1)}, f32[64,64]{0,1:T(8,128)S(1)}, u32[]{:S(2)}, u32[]{:S(2)}) collective-permute-start(f32[64,64]{0,1:T(8,128)S(1)} %slice_select_fusion.4), channel_id=1, source_target_pairs={{0,4},{4,0},{1,5},{5,1},{2,6},{6,2},{3,7},{7,3},{8,12},{12,8},{9,1... | collective-permute-start | bytes 49160 | tf_op jit(solution)/shard_map/ppermute | solution.py:16
  87.7 3.9 %collective-permute-start.16 = (f32[64,64]{0,1:T(8,128)S(1)}, f32[64,64]{0,1:T(8,128)S(1)}, u32[]{:S(2)}, u32[]{:S(2)}) collective-permute-start(f32[64,64]{0,1:T(8,128)S(1)} %maximum_select_fusion.12), channel_id=1, source_target_pairs={{0,4},{4,0},{1,5},{5,1},{2,6},{6,2},{3,7},{7,3},{8,12},{12,8},{9,1... | collective-permute-start | bytes 49160 | tf_op jit(solution)/shard_map/ppermute | solution.py:16
  91.7 4.3 %collective-permute-start.17 = (f32[64,128]{0,1:T(8,128)S(1)}, f32[64,128]{0,1:T(8,128)S(1)}, u32[]{:S(2)}, u32[]{:S(2)}) collective-permute-start(f32[64,128]{0,1:T(8,128)S(1)} %maximum_select_fusion.7), channel_id=1, source_target_pairs={{0,8},{8,0},{1,9},{9,1},{2,10},{10,2},{3,11},{11,3},{4,12},{12,4},... | collective-permute-start | bytes 98312 | tf_op jit(solution)/shard_map/ppermute | solution.py:16
  96.8 7.4 %collective-permute-start.18 = (f32[64,256]{0,1:T(8,128)S(1)}, f32[64,256]{0,1:T(8,128)S(1)}, u32[]{:S(2)}, u32[]{:S(2)}) collective-permute-start(f32[64,256]{0,1:T(8,128)S(1)} %slice_select_fusion), channel_id=1, source_target_pairs={{0,16},{16,0},{1,17},{17,1},{2,18},{18,2},{3,19},{19,3},{4,20},{20... | collective-permute-start | bytes 196616 | tf_op jit(solution)/shard_map/ppermute | solution.py:16
  104.3 4.3 %collective-permute-start.19 = (f32[64,128]{0,1:T(8,128)S(1)}, f32[64,128]{0,1:T(8,128)S(1)}, u32[]{:S(2)}, u32[]{:S(2)}) collective-permute-start(f32[64,128]{0,1:T(8,128)S(1)} %slice_select_fusion.1), channel_id=1, source_target_pairs={{0,8},{8,0},{1,9},{9,1},{2,10},{10,2},{3,11},{11,3},{4,12},{12,4},... | collective-permute-start | bytes 98312 | tf_op jit(solution)/shard_map/ppermute | solution.py:16
  108.6 4.0 %collective-permute-start.20 = (f32[64,64]{0,1:T(8,128)S(1)}, f32[64,64]{0,1:T(8,128)S(1)}, u32[]{:S(2)}, u32[]{:S(2)}) collective-permute-start(f32[64,64]{0,1:T(8,128)S(1)} %slice_select_fusion.3), channel_id=1, source_target_pairs={{0,4},{4,0},{1,5},{5,1},{2,6},{6,2},{3,7},{7,3},{8,12},{12,8},{9,1... | collective-permute-start | bytes 49160 | tf_op jit(solution)/shard_map/ppermute | solution.py:16
  122.6 3.9 %collective-permute-start.25 = (f32[64,64]{0,1:T(8,128)S(1)}, f32[64,64]{0,1:T(8,128)S(1)}, u32[]{:S(2)}, u32[]{:S(2)}) collective-permute-start(f32[64,64]{0,1:T(8,128)S(1)} %maximum_select_fusion.13), channel_id=1, source_target_pairs={{0,4},{4,0},{1,5},{5,1},{2,6},{6,2},{3,7},{7,3},{8,12},{12,8},{9,1... | collective-permute-start | bytes 49160 | tf_op jit(solution)/shard_map/ppermute | solution.py:16
  126.5 4.3 %collective-permute-start.26 = (f32[64,128]{0,1:T(8,128)S(1)}, f32[64,128]{0,1:T(8,128)S(1)}, u32[]{:S(2)}, u32[]{:S(2)}) collective-permute-start(f32[64,128]{0,1:T(8,128)S(1)} %maximum_select_fusion.8), channel_id=1, source_target_pairs={{0,8},{8,0},{1,9},{9,1},{2,10},{10,2},{3,11},{11,3},{4,12},{12,4},... | collective-permute-start | bytes 98312 | tf_op jit(solution)/shard_map/ppermute | solution.py:16
  130.9 7.1 %collective-permute-start.27 = (f32[64,256]{0,1:T(8,128)S(1)}, f32[64,256]{0,1:T(8,128)S(1)}, u32[]{:S(2)}, u32[]{:S(2)}) collective-permute-start(f32[64,256]{0,1:T(8,128)S(1)} %maximum_select_fusion.4), channel_id=1, source_target_pairs={{0,16},{16,0},{1,17},{17,1},{2,18},{18,2},{3,19},{19,3},{4,20},{20... | collective-permute-start | bytes 196616 | tf_op jit(solution)/shard_map/ppermute | solution.py:16
  140.0 5.6 %collective-permute-start.29 = (f32[64,512]{1,0:T(8,128)S(1)}, f32[64,512]{1,0:T(8,128)S(1)}, u32[]{:S(2)}, u32[]{:S(2)}) collective-permute-start(f32[64,512]{1,0:T(8,128)S(1)} %add.149), channel_id=1, source_target_pairs={{0,2},{2,0},{1,3},{3,1},{4,6},{6,4},{5,7},{7,5},{8,10},{10,8},{9,1... | collective-permute-start | bytes 393224 | tf_op jit(solution)/shard_map/ppermute | solution.py:16
  145.7 5.0 %collective-permute-start.30 = (f32[64,512]{1,0:T(8,128)S(1)}, f32[64,512]{1,0:T(8,128)S(1)}, u32[]{:S(2)}, u32[]{:S(2)}) collective-permute-start(f32[64,512]{1,0:T(8,128)S(1)} %add.150), channel_id=1, source_target_pairs={{0,4},{4,0},{1,5},{5,1},{2,6},{6,2},{3,7},{7,3},{8,12},{12,8},{9,1... | collective-permute-start | bytes 393224 | tf_op jit(solution)/shard_map/ppermute | solution.py:16
  150.7 5.0 %collective-permute-start.31 = (f32[64,512]{1,0:T(8,128)S(1)}, f32[64,512]{1,0:T(8,128)S(1)}, u32[]{:S(2)}, u32[]{:S(2)}) collective-permute-start(f32[64,512]{1,0:T(8,128)S(1)} %add.151), channel_id=1, source_target_pairs={{0,8},{8,0},{1,9},{9,1},{2,10},{10,2},{3,11},{11,3},{4,12},{12,4},... | collective-permute-start | bytes 393224 | tf_op jit(solution)/shard_map/ppermute | solution.py:16
  155.8 6.8 %collective-permute-start.32 = (f32[64,512]{1,0:T(8,128)S(1)}, f32[64,512]{1,0:T(8,128)S(1)}, u32[]{:S(2)}, u32[]{:S(2)}) collective-permute-start(f32[64,512]{1,0:T(8,128)S(1)} %add.152), channel_id=1, source_target_pairs={{0,16},{16,0},{1,17},{17,1},{2,18},{18,2},{3,19},{19,3},{4,20},{20... | collective-permute-start | bytes 393224 | tf_op jit(solution)/shard_map/ppermute | solution.py:16
  164.4 4.3 %collective-permute-start.34 = (f32[64,256]{1,0:T(8,128)S(1)}, f32[64,256]{1,0:T(8,128)S(1)}, u32[]{:S(2)}, u32[]{:S(2)}) collective-permute-start(f32[64,256]{1,0:T(8,128)S(1)} %add.154), channel_id=1, source_target_pairs={{0,2},{2,0},{1,3},{3,1},{4,6},{6,4},{5,7},{7,5},{8,10},{10,8},{9,1... | collective-permute-start | bytes 196616 | tf_op jit(solution)/shard_map/ppermute | solution.py:16
  168.8 4.3 %collective-permute-start.35 = (f32[64,256]{1,0:T(8,128)S(1)}, f32[64,256]{1,0:T(8,128)S(1)}, u32[]{:S(2)}, u32[]{:S(2)}) collective-permute-start(f32[64,256]{1,0:T(8,128)S(1)} %add.155), channel_id=1, source_target_pairs={{0,4},{4,0},{1,5},{5,1},{2,6},{6,2},{3,7},{7,3},{8,12},{12,8},{9,1... | collective-permute-start | bytes 196616 | tf_op jit(solution)/shard_map/ppermute | solution.py:16
  173.1 4.3 %collective-permute-start.36 = (f32[64,256]{1,0:T(8,128)S(1)}, f32[64,256]{1,0:T(8,128)S(1)}, u32[]{:S(2)}, u32[]{:S(2)}) collective-permute-start(f32[64,256]{1,0:T(8,128)S(1)} %add.156), channel_id=1, source_target_pairs={{0,8},{8,0},{1,9},{9,1},{2,10},{10,2},{3,11},{11,3},{4,12},{12,4},... | collective-permute-start | bytes 196616 | tf_op jit(solution)/shard_map/ppermute | solution.py:16
  179.2 3.9 %collective-permute-start.38 = (f32[64,128]{1,0:T(8,128)S(1)}, f32[64,128]{1,0:T(8,128)S(1)}, u32[]{:S(2)}, u32[]{:S(2)}) collective-permute-start(f32[64,128]{1,0:T(8,128)S(1)} %add.158), channel_id=1, source_target_pairs={{0,2},{2,0},{1,3},{3,1},{4,6},{6,4},{5,7},{7,5},{8,10},{10,8},{9,1... | collective-permute-start | bytes 98312 | tf_op jit(solution)/shard_map/ppermute | solution.py:16
  183.1 3.9 %collective-permute-start.39 = (f32[64,128]{1,0:T(8,128)S(1)}, f32[64,128]{1,0:T(8,128)S(1)}, u32[]{:S(2)}, u32[]{:S(2)}) collective-permute-start(f32[64,128]{1,0:T(8,128)S(1)} %add.159), channel_id=1, source_target_pairs={{0,4},{4,0},{1,5},{5,1},{2,6},{6,2},{3,7},{7,3},{8,12},{12,8},{9,1... | collective-permute-start | bytes 98312 | tf_op jit(solution)/shard_map/ppermute | solution.py:16
  188.7 3.9 %collective-permute-start.41 = (f32[64,64]{0,1:T(8,128)S(1)}, f32[64,64]{0,1:T(8,128)S(1)}, u32[]{:S(2)}, u32[]{:S(2)}) collective-permute-start(f32[64,64]{0,1:T(8,128)S(1)} %add.161), channel_id=1, source_target_pairs={{0,2},{2,0},{1,3},{3,1},{4,6},{6,4},{5,7},{7,5},{8,10},{10,8},{9,1... | collective-permute-start | bytes 49160 | tf_op jit(solution)/shard_map/ppermute | solution.py:16
  (29 other events, 568.2 us)
where the time goes:
time: 200 us; the launch traced here: 199 us
  waiting for transfers between devices  143 us (72%)
  starting transfers between devices  25 us (12%)
  matrix products  17.2 us (9%)
  local copies, waits for them, and re-layouts  7.1 us (4%)
  other arithmetic  5.52 us (3%)
    ppermute x42, waiting for transfers between devices, partner(): return lax.ppermute(block, axis, route)  132 us
    ppermute x42, starting transfers between devices, partner(): return lax.ppermute(block, axis, route)  14.9 us
    dot_general x9, matrix products, row_dot(): lax.dot_general(left, right, (((1,), (1,)), ((), ())), precision=HIGH)  8.69 us
    dot_general x10, matrix products, mat_dot(): return jnp.dot(left, right, precision=HIGH)  8.56 us
    all_to_all x1, starting transfers between devices, shards(): lax.all_to_all(send_rows, ('cube', 'front'), split_axis=1, concat_axis=1,...  7.33 us
    all_to_all x1, waiting for transfers between devices, shards(): lax.all_to_all(send_vals, ('cube', 'front'), split_axis=1, concat_axis=1,...  6.73 us
    all_to_all x1, waiting for transfers between devices, shards(): lax.all_to_all(send_rows, ('cube', 'front'), split_axis=1, concat_axis=1,...  4.08 us
  transfers between devices with their start and end apart: 44, of which 44 were waited for; matrix products, arithmetic and copies ran while one was open for 2% of the time, Pallas kernels for 0%

commit v1 on v0

--- a/solution.py
+++ b/solution.py
@@ -1,9 +1,22 @@
+import functools
 import jax
 import jax.numpy as jnp
 from jax import lax
 from jax.sharding import PartitionSpec as P
+from jax.lax import all_to_all, axis_size
 
 HIGH = lax.Precision.HIGHEST
+
+
+def _choose_circles(values, device_axis):
+    local_next = axis_size(device_axis)
+    w1 = jnp.split(values, local_next, 1)
+    w2 = jnp.stack(w1)
+    front = all_to_all(w2, device_axis, 0, 0)
+    return jnp.concatenate(front, 1)
+
+
+flows_make = functools.partial(_choose_circles, device_axis=("cube", "front"))
 
 
 def partner(block, axis, apart):
@@ -84,7 +97,7 @@
     send_rows = jnp.full((1, devices * capacity), -1, jnp.int32).at[0, slots].set(elem_row)
     got_vals, got_rows = (
         lax.all_to_all(send_vals, ("cube", "front"), split_axis=1, concat_axis=1, tiled=True),
-        lax.all_to_all(send_rows, ("cube", "front"), split_axis=1, concat_axis=1, tiled=True),
+        flows_make(send_rows),
     )
     placing = (got_rows[0][:, None] == jnp.arange(leaf_rows, dtype=jnp.int32)[None, :]).astype(
         jnp.float32

time: 200 us -> 217 us (1.085)
  local copies, waits for them, and re-layouts: 7.1 us -> 24.7 us
    unnamed x21 -> x52, local copies, waits for them, and re-layouts: 1.92 us -> 19.6 us
where the time goes in v1:
time: 217 us
  waiting for transfers between devices  143 us (66%)
  starting transfers between devices  25.1 us (12%)
  local copies, waits for them, and re-layouts  24.7 us (11%)
  matrix products  17.5 us (8%)
  other arithmetic  5.52 us (3%)
    ppermute x42, waiting for transfers between devices, partner(): return lax.ppermute(block, axis, route)  132 us
    unnamed x52, local copies, waits for them, and re-layouts  19.6 us
    ppermute x42, starting transfers between devices, partner(): return lax.ppermute(block, axis, route)  15 us
    dot_general x9, matrix products, row_dot(): lax.dot_general(left, right, (((1,), (1,)), ((), ())), precision=HIGH)  9 us
    dot_general x10, matrix products, mat_dot(): return jnp.dot(left, right, precision=HIGH)  8.47 us
    all_to_all x1, starting transfers between devices, _choose_circles(): front = all_to_all(w2, device_axis, 0, 0)  7.33 us
    all_to_all x1, waiting for transfers between devices, shards(): lax.all_to_all(send_vals, ('cube', 'front'), split_axis=1, concat_axis=1,...  6.73 us
  transfers between devices with their start and end apart: 44, of which 44 were waited for; matrix products, arithmetic and copies ran while one was open for 2% of the time, Pallas kernels for 0%

profile of v1, /device:TPU:0, one launch (start us, length us, event | category | flops | bytes accessed | tf_op | source)
XLA Modules:
  0.0 217.1 jit_solution(8135433554811807445)
XLA Ops:
  23.5 7.3 %all-to-all-start.1 = ((s32[32,1,16]{2,1,0:T(1,128)}), s32[32,1,16]{2,1,0:T(1,128)S(1)}, u32[]{:S(2)}, u32[]{:S(2)}) async-start(s32[32,1,16]{2,1,0:T(1,128)} %constant_dynamic-update-slice_fusion), calls=%async_computation.1 | async-start | bytes 32768 | tf_op jit(solution)/shard_map/all_to_all | solution.py:15
  33.9 4.1 %all-to-all-done.1 = s32[32,1,16]{2,1,0:T(1,128)S(1)} async-done(((s32[32,1,16]{2,1,0:T(1,128)}), s32[32,1,16]{2,1,0:T(1,128)S(1)}, u32[]{:S(2)}, u32[]{:S(2)}) %all-to-all-start.1) | async-done | bytes 2080 | tf_op jit(solution)/shard_map/all_to_all | solution.py:15
  42.0 6.7 %all-to-all-done = f32[32,1,1024]{2,1,0:T(1,128)S(1)} async-done(((f32[32,1,1024]{2,1,0:T(1,128)}), f32[32,1,1024]{2,1,0:T(1,128)S(1)}, u32[]{:S(2)}, u32[]{:S(2)}) %all-to-all-start) | async-done | bytes 131104 | tf_op jit(solution)/shard_map/all_to_all | solution.py:99
  51.4 6.3 %fusion.41 = f32[64,1024]{1,0:T(8,128)S(1)} fusion(f32[64,1024]{1,0:T(8,128)S(1)} %fusion, f32[1024,1024]{1,0:T(8,128)} %param.17), kind=kOutput, calls=%fused_computation.166 | convolution fusion | flops 805306368 | bytes 4718592 | tf_op jit(solution)/shard_map/dot_general | solution.py:33
  58.4 3.4 %collective-permute-done = f32[64,32]{0,1:T(8,128)S(1)} collective-permute-done((f32[64,32]{0,1:T(8,128)S(1)}, f32[64,32]{0,1:T(8,128)S(1)}, u32[]{:S(2)}, u32[]{:S(2)}) %collective-permute-start) | collective-permute-done | bytes 8224 | tf_op jit(solution)/shard_map/ppermute | solution.py:29
  64.7 3.4 %collective-permute-done.3 = f32[64,32]{0,1:T(8,128)S(1)} collective-permute-done((f32[64,32]{0,1:T(8,128)S(1)}, f32[64,32]{0,1:T(8,128)S(1)}, u32[]{:S(2)}, u32[]{:S(2)}) %collective-permute-start.3) | collective-permute-done | bytes 8224 | tf_op jit(solution)/shard_map/ppermute | solution.py:29
  72.9 3.4 %collective-permute-done.5 = f32[64,32]{0,1:T(8,128)S(1)} collective-permute-done((f32[64,32]{0,1:T(8,128)S(1)}, f32[64,32]{0,1:T(8,128)S(1)}, u32[]{:S(2)}, u32[]{:S(2)}) %collective-permute-start.5) | collective-permute-done | bytes 8224 | tf_op jit(solution)/shard_map/ppermute | solution.py:29
  79.1 3.4 %collective-permute-done.8 = f32[64,32]{0,1:T(8,128)S(1)} collective-permute-done((f32[64,32]{0,1:T(8,128)S(1)}, f32[64,32]{0,1:T(8,128)S(1)}, u32[]{:S(2)}, u32[]{:S(2)}) %collective-permute-start.8) | collective-permute-done | bytes 8224 | tf_op jit(solution)/shard_map/ppermute | solution.py:29
  87.7 3.6 %collective-permute-done.10 = f32[64,128]{0,1:T(8,128)S(1)} collective-permute-done((f32[64,128]{0,1:T(8,128)S(1)}, f32[64,128]{0,1:T(8,128)S(1)}, u32[]{:S(2)}, u32[]{:S(2)}) %collective-permute-start.10) | collective-permute-done | bytes 32800 | tf_op jit(solution)/shard_map/ppermute | solution.py:29
  110.0 3.6 %collective-permute-done.17 = f32[64,128]{0,1:T(8,128)S(1)} collective-permute-done((f32[64,128]{0,1:T(8,128)S(1)}, f32[64,128]{0,1:T(8,128)S(1)}, u32[]{:S(2)}, u32[]{:S(2)}) %collective-permute-start.17) | collective-permute-done | bytes 32800 | tf_op jit(solution)/shard_map/ppermute | solution.py:29
  115.3 6.5 %collective-permute-done.18 = f32[64,256]{0,1:T(8,128)S(1)} collective-permute-done((f32[64,256]{0,1:T(8,128)S(1)}, f32[64,256]{0,1:T(8,128)S(1)}, u32[]{:S(2)}, u32[]{:S(2)}) %collective-permute-start.18) | collective-permute-done | bytes 65568 | tf_op jit(solution)/shard_map/ppermute | solution.py:29
  122.0 4.3 %collective-permute-done.19 = f32[64,128]{0,1:T(8,128)S(1)} collective-permute-done((f32[64,128]{0,1:T(8,128)S(1)}, f32[64,128]{0,1:T(8,128)S(1)}, u32[]{:S(2)}, u32[]{:S(2)}) %collective-permute-start.19) | collective-permute-done | bytes 32800 | tf_op jit(solution)/shard_map/ppermute | solution.py:29
  144.2 4.3 %collective-permute-done.26 = f32[64,128]{0,1:T(8,128)S(1)} collective-permute-done((f32[64,128]{0,1:T(8,128)S(1)}, f32[64,128]{0,1:T(8,128)S(1)}, u32[]{:S(2)}, u32[]{:S(2)}) %collective-permute-start.26) | collective-permute-done | bytes 32800 | tf_op jit(solution)/shard_map/ppermute | solution.py:29
  148.6 7.0 %collective-permute-done.27 = f32[64,256]{0,1:T(8,128)S(1)} collective-permute-done((f32[64,256]{0,1:T(8,128)S(1)}, f32[64,256]{0,1:T(8,128)S(1)}, u32[]{:S(2)}, u32[]{:S(2)}) %collective-permute-start.27) | collective-permute-done | bytes 65568 | tf_op jit(solution)/shard_map/ppermute | solution.py:29
  158.3 5.2 %collective-permute-done.29 = f32[64,512]{1,0:T(8,128)S(1)} collective-permute-done((f32[64,512]{1,0:T(8,128)S(1)}, f32[64,512]{1,0:T(8,128)S(1)}, u32[]{:S(2)}, u32[]{:S(2)}) %collective-permute-start.29) | collective-permute-done | bytes 131104 | tf_op jit(solution)/shard_map/ppermute | solution.py:29
  164.2 4.3 %collective-permute-done.30 = f32[64,512]{1,0:T(8,128)S(1)} collective-permute-done((f32[64,512]{1,0:T(8,128)S(1)}, f32[64,512]{1,0:T(8,128)S(1)}, u32[]{:S(2)}, u32[]{:S(2)}) %collective-permute-start.30) | collective-permute-done | bytes 131104 | tf_op jit(solution)/shard_map/ppermute | solution.py:29
  168.7 5.0 %collective-permute-done.31 = f32[64,512]{1,0:T(8,128)S(1)} collective-permute-done((f32[64,512]{1,0:T(8,128)S(1)}, f32[64,512]{1,0:T(8,128)S(1)}, u32[]{:S(2)}, u32[]{:S(2)}) %collective-permute-start.31) | collective-permute-done | bytes 131104 | tf_op jit(solution)/shard_map/ppermute | solution.py:29
  173.7 6.7 %collective-permute-done.32 = f32[64,512]{1,0:T(8,128)S(1)} collective-permute-done((f32[64,512]{1,0:T(8,128)S(1)}, f32[64,512]{1,0:T(8,128)S(1)}, u32[]{:S(2)}, u32[]{:S(2)}) %collective-permute-start.32) | collective-permute-done | bytes 131104 | tf_op jit(solution)/shard_map/ppermute | solution.py:29
  182.8 3.9 %collective-permute-done.34 = f32[64,256]{1,0:T(8,128)S(1)} collective-permute-done((f32[64,256]{1,0:T(8,128)S(1)}, f32[64,256]{1,0:T(8,128)S(1)}, u32[]{:S(2)}, u32[]{:S(2)}) %collective-permute-start.34) | collective-permute-done | bytes 65568 | tf_op jit(solution)/shard_map/ppermute | solution.py:29
  187.4 3.6 %collective-permute-done.35 = f32[64,256]{1,0:T(8,128)S(1)} collective-permute-done((f32[64,256]{1,0:T(8,128)S(1)}, f32[64,256]{1,0:T(8,128)S(1)}, u32[]{:S(2)}, u32[]{:S(2)}) %collective-permute-start.35) | collective-permute-done | bytes 65568 | tf_op jit(solution)/shard_map/ppermute | solution.py:29
  191.1 4.3 %collective-permute-done.36 = f32[64,256]{1,0:T(8,128)S(1)} collective-permute-done((f32[64,256]{1,0:T(8,128)S(1)}, f32[64,256]{1,0:T(8,128)S(1)}, u32[]{:S(2)}, u32[]{:S(2)}) %collective-permute-start.36) | collective-permute-done | bytes 65568 | tf_op jit(solution)/shard_map/ppermute | solution.py:29
  197.4 3.5 %collective-permute-done.38 = f32[64,128]{1,0:T(8,128)S(1)} collective-permute-done((f32[64,128]{1,0:T(8,128)S(1)}, f32[64,128]{1,0:T(8,128)S(1)}, u32[]{:S(2)}, u32[]{:S(2)}) %collective-permute-start.38) | collective-permute-done | bytes 32800 | tf_op jit(solution)/shard_map/ppermute | solution.py:29
  207.1 3.4 %collective-permute-done.41 = f32[64,64]{0,1:T(8,128)S(1)} collective-permute-done((f32[64,64]{0,1:T(8,128)S(1)}, f32[64,64]{0,1:T(8,128)S(1)}, u32[]{:S(2)}, u32[]{:S(2)}) %collective-permute-start.41) | collective-permute-done | bytes 16416 | tf_op jit(solution)/shard_map/ppermute | solution.py:29
  210.9 5.5 %fusion.50 = f32[64,1024]{1,0:T(8,128)} fusion(f32[64,1024]{1,0:T(8,128)S(1)} %convolution_subtract_fusion, f32[1024,1024]{1,0:T(8,128)} %param.17), kind=kOutput, calls=%fused_computation.175 | convolution fusion | flops 805306368 | bytes 4718592 | tf_op jit(solution)/shard_map/dot_general | solution.py:37
  (211 shorter events, 103.3 us)
Async XLA Ops:
  23.5 14.4 %all-to-all-start.1 = ((s32[32,1,16]{2,1,0:T(1,128)}), s32[32,1,16]{2,1,0:T(1,128)S(1)}, u32[]{:S(2)}, u32[]{:S(2)}) async-start(s32[32,1,16]{2,1,0:T(1,128)} %constant_dynamic-update-slice_fusion), calls=%async_computation.1 | async-start | bytes 32768 | tf_op jit(solution)/shard_map/all_to_all | solution.py:15
  38.0 10.8 %all-to-all-start = ((f32[32,1,1024]{2,1,0:T(1,128)}), f32[32,1,1024]{2,1,0:T(1,128)S(1)}, u32[]{:S(2)}, u32[]{:S(2)}) async-start(f32[32,1,1024]{2,1,0:T(1,128)} %reshape.65), calls=%async_computation | async-start | bytes 262144 | tf_op jit(solution)/shard_map/all_to_all | solution.py:99
  68.5 4.0 %collective-permute-start.4 = (f32[64,64]{0,1:T(8,128)S(1)}, f32[64,64]{0,1:T(8,128)S(1)}, u32[]{:S(2)}, u32[]{:S(2)}) collective-permute-start(f32[64,64]{0,1:T(8,128)S(1)} %slice_select_fusion.5), channel_id=1, source_target_pairs={{0,4},{4,0},{1,5},{5,1},{2,6},{6,2},{3,7},{7,3},{8,12},{12,8},{9,1... | collective-permute-start | bytes 49160 | tf_op jit(solution)/shard_map/ppermute | solution.py:29
  82.5 3.9 %collective-permute-start.9 = (f32[64,64]{0,1:T(8,128)S(1)}, f32[64,64]{0,1:T(8,128)S(1)}, u32[]{:S(2)}, u32[]{:S(2)}) collective-permute-start(f32[64,64]{0,1:T(8,128)S(1)} %maximum_select_fusion.11), channel_id=1, source_target_pairs={{0,4},{4,0},{1,5},{5,1},{2,6},{6,2},{3,7},{7,3},{8,12},{12,8},{9,1... | collective-permute-start | bytes 49160 | tf_op jit(solution)/shard_map/ppermute | solution.py:29
  87.0 4.3 %collective-permute-start.10 = (f32[64,128]{0,1:T(8,128)S(1)}, f32[64,128]{0,1:T(8,128)S(1)}, u32[]{:S(2)}, u32[]{:S(2)}) collective-permute-start(f32[64,128]{0,1:T(8,128)S(1)} %slice_select_fusion.2), channel_id=1, source_target_pairs={{0,8},{8,0},{1,9},{9,1},{2,10},{10,2},{3,11},{11,3},{4,12},{12,4},... | collective-permute-start | bytes 98312 | tf_op jit(solution)/shard_map/ppermute | solution.py:29
  91.4 4.0 %collective-permute-start.11 = (f32[64,64]{0,1:T(8,128)S(1)}, f32[64,64]{0,1:T(8,128)S(1)}, u32[]{:S(2)}, u32[]{:S(2)}) collective-permute-start(f32[64,64]{0,1:T(8,128)S(1)} %slice_select_fusion.4), channel_id=1, source_target_pairs={{0,4},{4,0},{1,5},{5,1},{2,6},{6,2},{3,7},{7,3},{8,12},{12,8},{9,1... | collective-permute-start | bytes 49160 | tf_op jit(solution)/shard_map/ppermute | solution.py:29
  105.4 3.9 %collective-permute-start.16 = (f32[64,64]{0,1:T(8,128)S(1)}, f32[64,64]{0,1:T(8,128)S(1)}, u32[]{:S(2)}, u32[]{:S(2)}) collective-permute-start(f32[64,64]{0,1:T(8,128)S(1)} %maximum_select_fusion.12), channel_id=1, source_target_pairs={{0,4},{4,0},{1,5},{5,1},{2,6},{6,2},{3,7},{7,3},{8,12},{12,8},{9,1... | collective-permute-start | bytes 49160 | tf_op jit(solution)/shard_map/ppermute | solution.py:29
  109.3 4.3 %collective-permute-start.17 = (f32[64,128]{0,1:T(8,128)S(1)}, f32[64,128]{0,1:T(8,128)S(1)}, u32[]{:S(2)}, u32[]{:S(2)}) collective-permute-start(f32[64,128]{0,1:T(8,128)S(1)} %maximum_select_fusion.7), channel_id=1, source_target_pairs={{0,8},{8,0},{1,9},{9,1},{2,10},{10,2},{3,11},{11,3},{4,12},{12,4},... | collective-permute-start | bytes 98312 | tf_op jit(solution)/shard_map/ppermute | solution.py:29
  114.5 7.4 %collective-permute-start.18 = (f32[64,256]{0,1:T(8,128)S(1)}, f32[64,256]{0,1:T(8,128)S(1)}, u32[]{:S(2)}, u32[]{:S(2)}) collective-permute-start(f32[64,256]{0,1:T(8,128)S(1)} %slice_select_fusion), channel_id=1, source_target_pairs={{0,16},{16,0},{1,17},{17,1},{2,18},{18,2},{3,19},{19,3},{4,20},{20... | collective-permute-start | bytes 196616 | tf_op jit(solution)/shard_map/ppermute | solution.py:29
  121.9 4.3 %collective-permute-start.19 = (f32[64,128]{0,1:T(8,128)S(1)}, f32[64,128]{0,1:T(8,128)S(1)}, u32[]{:S(2)}, u32[]{:S(2)}) collective-permute-start(f32[64,128]{0,1:T(8,128)S(1)} %slice_select_fusion.1), channel_id=1, source_target_pairs={{0,8},{8,0},{1,9},{9,1},{2,10},{10,2},{3,11},{11,3},{4,12},{12,4},... | collective-permute-start | bytes 98312 | tf_op jit(solution)/shard_map/ppermute | solution.py:29
  126.2 4.0 %collective-permute-start.20 = (f32[64,64]{0,1:T(8,128)S(1)}, f32[64,64]{0,1:T(8,128)S(1)}, u32[]{:S(2)}, u32[]{:S(2)}) collective-permute-start(f32[64,64]{0,1:T(8,128)S(1)} %slice_select_fusion.3), channel_id=1, source_target_pairs={{0,4},{4,0},{1,5},{5,1},{2,6},{6,2},{3,7},{7,3},{8,12},{12,8},{9,1... | collective-permute-start | bytes 49160 | tf_op jit(solution)/shard_map/ppermute | solution.py:29
  140.2 3.9 %collective-permute-start.25 = (f32[64,64]{0,1:T(8,128)S(1)}, f32[64,64]{0,1:T(8,128)S(1)}, u32[]{:S(2)}, u32[]{:S(2)}) collective-permute-start(f32[64,64]{0,1:T(8,128)S(1)} %maximum_select_fusion.13), channel_id=1, source_target_pairs={{0,4},{4,0},{1,5},{5,1},{2,6},{6,2},{3,7},{7,3},{8,12},{12,8},{9,1... | collective-permute-start | bytes 49160 | tf_op jit(solution)/shard_map/ppermute | solution.py:29
  144.2 4.3 %collective-permute-start.26 = (f32[64,128]{0,1:T(8,128)S(1)}, f32[64,128]{0,1:T(8,128)S(1)}, u32[]{:S(2)}, u32[]{:S(2)}) collective-permute-start(f32[64,128]{0,1:T(8,128)S(1)} %maximum_select_fusion.8), channel_id=1, source_target_pairs={{0,8},{8,0},{1,9},{9,1},{2,10},{10,2},{3,11},{11,3},{4,12},{12,4},... | collective-permute-start | bytes 98312 | tf_op jit(solution)/shard_map/ppermute | solution.py:29
  148.5 7.1 %collective-permute-start.27 = (f32[64,256]{0,1:T(8,128)S(1)}, f32[64,256]{0,1:T(8,128)S(1)}, u32[]{:S(2)}, u32[]{:S(2)}) collective-permute-start(f32[64,256]{0,1:T(8,128)S(1)} %maximum_select_fusion.4), channel_id=1, source_target_pairs={{0,16},{16,0},{1,17},{17,1},{2,18},{18,2},{3,19},{19,3},{4,20},{20... | collective-permute-start | bytes 196616 | tf_op jit(solution)/shard_map/ppermute | solution.py:29
  157.9 5.6 %collective-permute-start.29 = (f32[64,512]{1,0:T(8,128)S(1)}, f32[64,512]{1,0:T(8,128)S(1)}, u32[]{:S(2)}, u32[]{:S(2)}) collective-permute-start(f32[64,512]{1,0:T(8,128)S(1)} %add.149), channel_id=1, source_target_pairs={{0,2},{2,0},{1,3},{3,1},{4,6},{6,4},{5,7},{7,5},{8,10},{10,8},{9,1... | collective-permute-start | bytes 393224 | tf_op jit(solution)/shard_map/ppermute | solution.py:29
  163.5 5.0 %collective-permute-start.30 = (f32[64,512]{1,0:T(8,128)S(1)}, f32[64,512]{1,0:T(8,128)S(1)}, u32[]{:S(2)}, u32[]{:S(2)}) collective-permute-start(f32[64,512]{1,0:T(8,128)S(1)} %add.150), channel_id=1, source_target_pairs={{0,4},{4,0},{1,5},{5,1},{2,6},{6,2},{3,7},{7,3},{8,12},{12,8},{9,1... | collective-permute-start | bytes 393224 | tf_op jit(solution)/shard_map/ppermute | solution.py:29
  168.6 5.0 %collective-permute-start.31 = (f32[64,512]{1,0:T(8,128)S(1)}, f32[64,512]{1,0:T(8,128)S(1)}, u32[]{:S(2)}, u32[]{:S(2)}) collective-permute-start(f32[64,512]{1,0:T(8,128)S(1)} %add.151), channel_id=1, source_target_pairs={{0,8},{8,0},{1,9},{9,1},{2,10},{10,2},{3,11},{11,3},{4,12},{12,4},... | collective-permute-start | bytes 393224 | tf_op jit(solution)/shard_map/ppermute | solution.py:29
  173.6 6.8 %collective-permute-start.32 = (f32[64,512]{1,0:T(8,128)S(1)}, f32[64,512]{1,0:T(8,128)S(1)}, u32[]{:S(2)}, u32[]{:S(2)}) collective-permute-start(f32[64,512]{1,0:T(8,128)S(1)} %add.152), channel_id=1, source_target_pairs={{0,16},{16,0},{1,17},{17,1},{2,18},{18,2},{3,19},{19,3},{4,20},{20... | collective-permute-start | bytes 393224 | tf_op jit(solution)/shard_map/ppermute | solution.py:29
  182.3 4.3 %collective-permute-start.34 = (f32[64,256]{1,0:T(8,128)S(1)}, f32[64,256]{1,0:T(8,128)S(1)}, u32[]{:S(2)}, u32[]{:S(2)}) collective-permute-start(f32[64,256]{1,0:T(8,128)S(1)} %add.154), channel_id=1, source_target_pairs={{0,2},{2,0},{1,3},{3,1},{4,6},{6,4},{5,7},{7,5},{8,10},{10,8},{9,1... | collective-permute-start | bytes 196616 | tf_op jit(solution)/shard_map/ppermute | solution.py:29
  186.6 4.3 %collective-permute-start.35 = (f32[64,256]{1,0:T(8,128)S(1)}, f32[64,256]{1,0:T(8,128)S(1)}, u32[]{:S(2)}, u32[]{:S(2)}) collective-permute-start(f32[64,256]{1,0:T(8,128)S(1)} %add.155), channel_id=1, source_target_pairs={{0,4},{4,0},{1,5},{5,1},{2,6},{6,2},{3,7},{7,3},{8,12},{12,8},{9,1... | collective-permute-start | bytes 196616 | tf_op jit(solution)/shard_map/ppermute | solution.py:29
  191.0 4.3 %collective-permute-start.36 = (f32[64,256]{1,0:T(8,128)S(1)}, f32[64,256]{1,0:T(8,128)S(1)}, u32[]{:S(2)}, u32[]{:S(2)}) collective-permute-start(f32[64,256]{1,0:T(8,128)S(1)} %add.156), channel_id=1, source_target_pairs={{0,8},{8,0},{1,9},{9,1},{2,10},{10,2},{3,11},{11,3},{4,12},{12,4},... | collective-permute-start | bytes 196616 | tf_op jit(solution)/shard_map/ppermute | solution.py:29
  197.0 3.9 %collective-permute-start.38 = (f32[64,128]{1,0:T(8,128)S(1)}, f32[64,128]{1,0:T(8,128)S(1)}, u32[]{:S(2)}, u32[]{:S(2)}) collective-permute-start(f32[64,128]{1,0:T(8,128)S(1)} %add.158), channel_id=1, source_target_pairs={{0,2},{2,0},{1,3},{3,1},{4,6},{6,4},{5,7},{7,5},{8,10},{10,8},{9,1... | collective-permute-start | bytes 98312 | tf_op jit(solution)/shard_map/ppermute | solution.py:29
  201.0 3.9 %collective-permute-start.39 = (f32[64,128]{1,0:T(8,128)S(1)}, f32[64,128]{1,0:T(8,128)S(1)}, u32[]{:S(2)}, u32[]{:S(2)}) collective-permute-start(f32[64,128]{1,0:T(8,128)S(1)} %add.159), channel_id=1, source_target_pairs={{0,4},{4,0},{1,5},{5,1},{2,6},{6,2},{3,7},{7,3},{8,12},{12,8},{9,1... | collective-permute-start | bytes 98312 | tf_op jit(solution)/shard_map/ppermute | solution.py:29
  206.6 3.9 %collective-permute-start.41 = (f32[64,64]{0,1:T(8,128)S(1)}, f32[64,64]{0,1:T(8,128)S(1)}, u32[]{:S(2)}, u32[]{:S(2)}) collective-permute-start(f32[64,64]{0,1:T(8,128)S(1)} %add.161), channel_id=1, source_target_pairs={{0,2},{2,0},{1,3},{3,1},{4,6},{6,4},{5,7},{7,5},{8,10},{10,8},{9,1... | collective-permute-start | bytes 49160 | tf_op jit(solution)/shard_map/ppermute | solution.py:29
  (29 other events, 638.7 us)
